TPU v7x, 512 devices: a whole 4x8x8 slice. The times are simulated.
512 devices in a mesh: member: 16 (over x, y_lo), space: 16 (over z, core), dp: 2 (over y_hi).
Axes of the slice: x: 4, y: 8 (y_hi: 2, y_lo: 4; y = y_hi * 4 + y_lo), z: 8, core: 2. Of those that a mesh axis runs over, the one named last changes fastest.
Arguments:
- latent: bfloat16 [16, 2, 16384, 1024], P('member', 'dp', 'space'), may hold values from -6 to 6
- target: bfloat16 [2, 100, 16384], P('dp', None, 'space'), may hold values from -6 to 6
- weight: bfloat16 [100, 1024], replicated, may hold values from -0.1875 to 0.1875
- bias: float32 [100], replicated, may hold values from -3 to 3
- gain: float32 [1024], replicated, may hold values from 0.1 to 1.9
- channel_weight: float32 [100], replicated, may hold values from 0.25 to 4
- band_offsets: int32 [17], replicated, may hold values from 0 to 80, as said below
- row_points: int32 [128], replicated, may hold values from 64 to 128, as said below
Outputs:
- grad_latent: bfloat16 [16, 2, 16384, 1024], P('member', 'dp', 'space')
- grad_weight: float32 [100, 1024], replicated
- grad_bias: float32 [100], replicated
- grad_gain: float32 [1024], replicated
- loss: float32 [], replicated
Inputs may be any that keep to these rules, and one draw needn't show every extreme that they name: `band_offsets`: nondecreasing, starting at 0; band s holds rows band_offsets[s] to band_offsets[s+1] - 1, at least 2 and at most 8 rows, and its points fill its first slots. `row_points`: the rows of one band hold at most 1024 points together, exactly 1024 in some band.
All inputs are finite; a program needn't handle non-finite values.
Results may differ from a plain program's by a relative error of at most 0.0084.
Values sent between devices are 32-bit elements; how exact they have to be, the bound alone decides.
A program may use at most 64 MiB of HBM per device.

v0:
```python
import jax
import jax.numpy as jnp
from jax import lax
from jax.sharding import PartitionSpec as P

smooth_sq = 0.01


def smooth_abs(value):
    return jnp.sqrt(value * value + smooth_sq)


def smooth_sign(value):
    return value / jnp.sqrt(value * value + smooth_sq)


def normalize(samples, gain):
    values = samples.astype(jnp.float32)
    middle = jnp.mean(values, axis=-1, keepdims=True)
    centered = values - middle
    variance = jnp.mean(centered * centered, axis=-1, keepdims=True)
    inverse = lax.rsqrt(variance + 1e-05)
    unit_rows = centered * inverse
    scaled = (unit_rows * gain).astype(jnp.bfloat16)
    return (unit_rows, inverse, scaled)


def shards(latent, target, weight, bias, gain, channel_weight, band_offsets, row_points):
    members = lax.axis_size("member")
    bands = lax.axis_size("space")
    band = lax.axis_index("space")
    own_member = lax.axis_index("member")
    row_ids = jnp.arange(row_points.shape[0], dtype=jnp.int32)
    in_band = (row_ids[None, :] >= band_offsets[:-1, None]) & (
        row_ids[None, :] < band_offsets[1:, None]
    )
    counts = jnp.sum(jnp.where(in_band, row_points[None, :], 0), axis=1)
    live_count = jnp.sum(jnp.where(jnp.arange(bands, dtype=jnp.int32) == band, counts, 0))
    total_live = jnp.sum(counts).astype(jnp.float32)
    samples = latent[0]
    slots = samples.shape[1]
    live = (jnp.arange(slots, dtype=jnp.int32) < live_count).astype(jnp.float32)
    unit_rows, inverse, scaled = normalize(samples, gain)
    predicted = (
        jnp.einsum("bph,ch->bcp", scaled, weight, preferred_element_type=jnp.float32)
        + bias[None, :, None]
    )
    grid_weight = channel_weight[None, :, None] * live[None, None, :]
    error = predicted - target.astype(jnp.float32)
    skill = jnp.sum(grid_weight * smooth_abs(error))
    pair_weight = 1.0 / (members - 1)
    piece = lax.all_gather(predicted[None], "member", axis=0, tiled=True)
    count = piece.shape[0]
    others = (jnp.arange(count, dtype=jnp.int32) != own_member).astype(jnp.float32)[
        :, None, None, None
    ]
    spread_gap = predicted[None] - piece
    spread_sum = jnp.sum(grid_weight[None] * others * smooth_abs(spread_gap))
    slope_sum = jnp.sum(others * smooth_sign(spread_gap), axis=0)
    local_score = skill - 0.5 * pair_weight * spread_sum
    dpred = grid_weight * (smooth_sign(error) - pair_weight * slope_sum)
    dpred_low = dpred.astype(jnp.bfloat16)
    grad_w = jnp.einsum("bcp,bph->ch", dpred_low, scaled, preferred_element_type=jnp.float32)
    grad_b = jnp.sum(dpred, axis=(0, 2))
    dscaled = jnp.einsum("bcp,ch->bph", dpred_low, weight, preferred_element_type=jnp.float32)
    grad_g = jnp.sum(dscaled * unit_rows, axis=(0, 1))
    dunit = dscaled * gain
    first = jnp.mean(dunit, axis=-1, keepdims=True)
    second = jnp.mean(dunit * unit_rows, axis=-1, keepdims=True)
    grad_x = (inverse * (dunit - first - unit_rows * second)).astype(jnp.bfloat16)
    sum_w, sum_b, sum_g, sum_score = lax.psum(
        (grad_w, grad_b, grad_g, local_score), ("member", "space", "dp")
    )
    batch = samples.shape[0] * lax.axis_size("dp")
    loss = sum_score / (weight.shape[0] * batch * total_live)
    return (grad_x[None], sum_w, sum_b, sum_g, loss)


def solution(mesh):
    return jax.shard_map(
        shards,
        mesh=mesh,
        in_specs=(
            P("member", "dp", "space", None),
            P("dp", None, "space"),
            P(),
            P(),
            P(),
            P(),
            P(),
            P(),
        ),
        out_specs=(P("member", "dp", "space", None), P(), P(), P(), P()),
        check_vma=False,
    )
```

profile of v0, /device:TPU:1, one launch (start us, length us, event | category | flops | bytes accessed | tf_op | source)
XLA Modules:
  0.0 467.6 jit_solution(11264365382467686688)
XLA Ops:
  7.2 0.0 copy-start
  7.2 0.0 copy-start.3
  7.2 0.0 copy-start.7
  7.2 0.0 all-gather.4.cloned.1.call-start
  7.2 2.9 copy.17
  10.2 0.4 convert_reduce_fusion
  10.5 0.0 copy-start.5
  10.5 0.0 copy-start.6
  10.6 0.0 copy-start.4
  10.6 0.6 fusion.2
  11.2 0.0 copy-done
  11.2 0.0 copy-done.3
  11.2 0.0 copy-done.7
  11.2 1.6 fusion.30
  12.8 0.0 all-gather.4.cloned.1.call-update
  12.8 0.0 all-reduce.3.cloned.1.call-start
  12.9 0.0 copy-done.5
  12.9 0.1 fusion.43
  12.9 0.0 copy-done.6
  13.0 0.7 select_reduce_fusion
  14.3 0.6 fusion.41
  15.0 0.6 fusion.40
  15.6 0.0 copy-done.4
  15.6 0.0 copy-start.1
  15.6 0.0 copy-start.2
  15.6 0.1 broadcast_multiply_fusion
  15.8 159.0 %all-gather.4.cloned.1.call-done = f32[16,100,1024]{2,1,0:T(8,128)} async-done(((f32[1,100,1024]{2,1,0:T(8,128)}), f32[16,100,1024]{2,1,0:T(8,128)}) %all-gather.4.cloned.1.call-update) | async-done | bytes 6553616 | tf_op jit(solution)/shard_map/all_gather | solution.py:52
  174.8 6.8 %multiply_reduce_fusion = (f32[]{:T(128)}, f32[100,1024]{1,0:T(8,128)S(1)}) fusion(f32[16,100,1024]{2,1,0:T(8,128)} %all-gather.4.cloned.1.call-done, f32[100,1024]{1,0:T(8,128)S(1)} %broadcast_multiply_fusion, f32[100,1024]{1,0:T(8,128)} %bitcast.71, f32[16]{0:T(128)S(1)} %compare_convert_fusion), kind=kLoop, calls=%fused_computation.5 | loop fusion | flops 14643199 | bytes 7782468 | tf_op jit(solution)/shard_map/reduce_sum | solution.py:58
  181.5 0.0 copy-done.1
  181.5 0.0 copy-done.2
  181.5 1.0 fusion.42
  182.5 1.6 fusion.22
  184.2 3.4 fusion.17
  187.6 0.0 all-reduce.3.cloned.1.call-update
  187.6 4.7 %fusion.18 = bf16[1,1,1024,1024]{2,3,1,0:T(8,128)(2,1)} fusion(bf16[1,1,1024,1024]{2,3,1,0:T(8,128)(2,1)S(1)} %copy.17, f32[1024,1024]{0,1:T(8,128)} %get-tuple-element.35, f32[1024]{0:T(1024)S(1)} %get-tuple-element.36, f32[1024]{0:T(1024)S(1)} %get-tuple-element.37, f32[1024]{0:T(1024)S(1)} %copy-done.3, f32[1024]{0:T(1024)S(1)} %broadcast_multiply_fusion.3, ...), kind=kLoop, calls=%fused_computation.27 | loop fusion | flops 9437184 | bytes 8409088 | tf_op jit(solution)/shard_map/broadcast_in_dim | solution.py:76
  192.3 3.9 copy.18
  197.6 99.5 %all-reduce = (f32[100]{0:T(128)}, f32[1024]{0:T(1024)}, f32[]{:T(128)}) all-reduce(f32[100]{0:T(128)S(1)} %get-tuple-element.30, f32[1024]{0:T(1024)S(1)} %get-tuple-element.22, f32[]{:T(128)S(6)} %sub.72), channel_id=1, replica_groups=mesh['member'=16,'space'=16,'dp'=2] {'member','space','dp'}, use_global_device_ids=true, to_apply=%region_9.10 | all-reduce | flops 1125 | bytes 9000 | tf_op jit(solution)/shard_map/psum | solution.py:71
  297.7 160.1 %all-reduce.3.cloned.1.call-done = f32[100,1024]{1,0:T(8,128)} async-done(((f32[100,1024]{1,0:T(8,128)}), f32[100,1024]{1,0:T(8,128)}) %all-reduce.3.cloned.1.call-update) | async-done | bytes 409616 | tf_op jit(solution)/shard_map/psum | solution.py:71
  457.8 1.8 copy.20
  (4 shorter events, 0.0 us)
Async XLA Ops:
  7.2 4.0 copy-start
  7.2 4.0 copy-start.3
  7.2 4.0 copy-start.7
  7.2 167.6 %all-gather.4.cloned.1.call-start = ((), (), s32[]{:S(2)}) async-start(), calls=%async_computation.1 | async-start | bytes 7241728 | tf_op jit(solution)/shard_map/all_gather | solution.py:52
  10.5 2.3 copy-start.5
  10.5 2.4 copy-start.6
  10.6 5.1 %copy-start.4 = (f32[100]{0:T(128)S(1)}, f32[100]{0:T(128)}, u32[]{:S(2)}) copy-start(f32[100]{0:T(128)} %param.13) | copy-start | bytes 1204
  12.8 445.0 %all-reduce.3.cloned.1.call-start = ((), (), s32[]{:S(2)}) async-start(), calls=%async_computation | async-start | bytes 851968 | tf_op jit(solution)/shard_map/psum | solution.py:71
  15.6 165.9 %copy-start.1 = (f32[1024,100]{0,1:T(8,128)S(1)}, f32[1024,100]{0,1:T(8,128)}, u32[]{:S(2)}) copy-start(f32[1024,100]{0,1:T(8,128)} %fusion.30) | copy-start | bytes 1228804
  15.6 165.9 %copy-start.2 = (bf16[1,100,1024]{2,1,0:T(8,128)(2,1)S(1)}, bf16[1,100,1024]{2,1,0:T(8,128)(2,1)}, u32[]{:S(2)}) copy-start(bf16[1,100,1024]{2,1,0:T(8,128)(2,1)} %param.9) | copy-start | bytes 614404
Sparse Core Ops, SparseCore 0:
  12.9 161.7 all-gather.3
  187.7 270.0 all-reduce.2
where the time goes:
time: 468 us
  waiting for transfers between devices  319 us (68%)
  blocking collectives  99.5 us (21%)
  between operations  17.9 us (4%)
  other arithmetic  15.5 us (3%)
  local copies, waits for them, and re-layouts  8.76 us (2%)
  matrix products  6.64 us (1%)
    psum x1, waiting for transfers between devices, shards(): lax.psum((grad_w, grad_b, grad_g, local_score), ('member', 'space', 'dp'))  160 us
    all_gather x1, waiting for transfers between devices, shards(): piece = lax.all_gather(predicted[None], 'member', axis=0, tiled=True)  159 us
    psum x1, blocking collectives, shards(): lax.psum((grad_w, grad_b, grad_g, local_score), ('member', 'space', 'dp'))  99.5 us
  transfers between devices with their start and end apart: 2, of which 2 were waited for; matrix products, arithmetic and copies ran while one was open for 2% of the time, Pallas kernels for 0%

commit v1 on v0

v1 whole, which is shorter than its diff:
```python
import jax
import jax.numpy as jnp
from jax import lax
from jax.experimental import pallas as pl
from jax.experimental.pallas import tpu as pltpu
from jax.sharding import PartitionSpec as P

MESH = pl.DeviceIdType.MESH
F32 = jnp.float32
BF16 = jnp.bfloat16
H, C, PTS = 1024, 100, 1024
MEMBERS, NX, NY, NZ, YLO = 16, 4, 8, 8, 4
HALF, LANES, BLOCKS = 56, 128, 8
SMOOTH = 0.01


def remote(src, dst, send, recv, where):
    return pltpu.make_async_remote_copy(
        src_ref=src, dst_ref=dst, send_sem=send, recv_sem=recv, device_id=where, device_id_type=MESH
    )


def kernel(
    lat, tgt, weight, bias, gain, chan, live,
    out_lat, out_w, out_g, out_x,
    wpad, wgain, bcol, qcol, rows, tpad, bsum,
    scaled, s_mean, s_inv, pred, got, back, grads, dlow,
    full, r_core, sum_core, r_x, sum_x, r_y, sum_y, r_z, final,
    a_send, a_recv, b_send, b_recv, c_sem, x_send, x_recv, y_send, y_recv,
    z_send, z_recv, gy_send, gy_recv, gx_send, gx_recv, gc_sem,
):
    me = lax.axis_index("member")
    sp = lax.axis_index("space")
    dp = lax.axis_index("dp")
    my_x, y_lo = me // YLO, me % YLO
    my_y = dp * YLO + y_lo
    my_z, core = sp // 2, sp % 2
    far = (dp + 1) % 2
    mate = my_z * 2 + (1 - core)
    block, half = me // 2, me % 2

    barrier = pltpu.get_barrier_semaphore()

    @pl.loop(1, MEMBERS)
    def _(i):
        pl.semaphore_signal(barrier, inc=1, device_id={"member": (me + i) % MEMBERS}, device_id_type=MESH)

    @pl.loop(0, YLO)
    def _(i):
        pl.semaphore_signal(
            barrier, inc=1, device_id={"member": my_x * YLO + i, "dp": far}, device_id_type=MESH
        )

    @pl.loop(1, NZ)
    def _(i):
        pl.semaphore_signal(
            barrier, inc=1, device_id={"space": ((my_z + i) % NZ) * 2 + core}, device_id_type=MESH
        )

    pl.semaphore_signal(barrier, inc=1, device_id={"space": mate}, device_id_type=MESH)

    wpad[96:128, :] = jnp.zeros((32, H), BF16)
    wpad[0:C, :] = weight[...]
    rows[...] = jnp.zeros((16, LANES), F32)
    rows[0:1, 0:C] = bias[...]
    rows[8:9, 0:C] = chan[...]
    bcol[...] = jnp.transpose(jnp.broadcast_to(rows[0:1, :], (LANES, LANES)))
    qcol[...] = jnp.transpose(jnp.broadcast_to(rows[8:9, :], (LANES, LANES)))
    pl.semaphore_wait(barrier, (MEMBERS - 1) + YLO + (NZ - 1) + 1)

    @pl.loop(0, BLOCKS)
    def _(i):
        j = (block + 1 + i) % BLOCKS
        pts = pl.ds(pl.multiple_of(j * LANES, LANES), LANES)
        values = lat[pts, :].astype(F32)
        mean = jnp.sum(values, axis=1, keepdims=True) * (1.0 / H)
        centered = values - mean
        var = jnp.sum(centered * centered, axis=1, keepdims=True) * (1.0 / H)
        inv = lax.rsqrt(var + 1e-05)
        low = ((centered * inv) * gain[...]).astype(BF16)
        scaled[pts, :] = low
        s_mean[pts, :] = mean
        s_inv[pts, :] = inv
        out = lax.dot_general(
            wpad[0 : 2 * HALF, :], low, (((1,), (1,)), ((), ())), preferred_element_type=F32
        )
        out = out + bcol[0 : 2 * HALF, :]
        for r in range(2):
            k = 2 * j + r
            pred[k] = out[r * HALF : (r + 1) * HALF]

            @pl.when(k != me)
            def _():
                remote(pred.at[k], got.at[me], a_send.at[k], a_recv.at[me], {"member": k}).start()

    mine = pl.ds(pl.multiple_of(block * LANES, LANES), LANES)
    tpad[96:112, :] = jnp.zeros((16, LANES), F32)
    tpad[0:C, :] = tgt[:, mine].astype(F32)
    bsum[...] = jnp.zeros((LANES, LANES), F32)
    got[me] = pred[me]

    wg = wpad[...].astype(F32) * gain[...]
    wgain[...] = (wg - jnp.sum(wg, axis=1, keepdims=True) * (1.0 / H)).astype(BF16)

    @pl.loop(1, MEMBERS)
    def _(i):
        k = (me + i) % MEMBERS
        remote(pred.at[k], got.at[k], a_send.at[k], a_recv.at[k], {"member": k}).wait()

    live_row = live[0:1, mine]
    pair = 1.0 / (MEMBERS - 1)

    def tile(t, score):
        row = pl.multiple_of(t * 8, 8)
        here = pl.ds(row, 8)
        band = pl.ds(pl.multiple_of(half * HALF + row, 8), 8)
        q = qcol[band, :] * live_row
        obs = tpad[band, :]
        p = [got[m, here, :] for m in range(MEMBERS)]
        slope = [None] * MEMBERS
        spread = jnp.zeros((8, LANES), F32)
        for m in range(MEMBERS):
            for n in range(m + 1, MEMBERS):
                gap = p[m] - p[n]
                square = gap * gap + SMOOTH
                root = lax.rsqrt(square)
                spread = spread + square * root
                sign = gap * root
                slope[m] = sign if slope[m] is None else slope[m] + sign
                slope[n] = -sign if slope[n] is None else slope[n] - sign
        skill = jnp.zeros((8, LANES), F32)
        total = jnp.zeros((8, LANES), F32)
        for m in range(MEMBERS):
            gap = p[m] - obs
            square = gap * gap + SMOOTH
            root = lax.rsqrt(square)
            skill = skill + square * root
            sign = gap * root
            total = total + sign
            back[m, here, :] = q * (sign - pair * slope[m])
        bsum[band, :] = q * total
        return score + q * (skill - pair * spread)

    score = lax.fori_loop(0, HALF // 8, tile, jnp.zeros((8, LANES), F32))
    score = jnp.sum(jnp.sum(score, axis=1, keepdims=True), axis=0, keepdims=True)

    @pl.loop(1, MEMBERS)
    def _(i):
        k = (me + i) % MEMBERS
        remote(back.at[k], grads.at[me], b_send.at[k], b_recv.at[me], {"member": k}).start()

    grads[me] = back[me]
    bias_row = jnp.sum(jnp.transpose(bsum[...]), axis=0, keepdims=True)
    row_id = lax.broadcasted_iota(jnp.int32, (16, LANES), 0)
    for y in range(NY):
        full[1, 3, y] = jnp.zeros((16, LANES), F32)
    full[1, 3, 0] = jnp.where(row_id == 0, bias_row, jnp.where(row_id == 1, score, 0.0))

    @pl.loop(1, MEMBERS)
    def _(i):
        k = (me + i) % MEMBERS
        remote(back.at[k], grads.at[k], b_send.at[k], b_recv.at[k], {"member": k}).wait()

    for j in range(BLOCKS):
        pts = slice(j * LANES, (j + 1) * LANES)
        dlow[0:HALF, pts] = grads[2 * j]
        dlow[HALF : 2 * HALF, pts] = grads[2 * j + 1]

    dl = dlow[...].astype(BF16)
    for y in range(NY):
        gw = jnp.dot(dl, scaled[:, y * LANES : (y + 1) * LANES], preferred_element_type=F32)
        for g in range(7):
            full[g // 4, g % 4, y] = gw[g * 16 : (g + 1) * 16]

    core_copy = remote(full.at[1 - core], r_core, c_sem.at[0], c_sem.at[1], {"space": mate})
    core_copy.start()

    def latent_block(j):
        pts = pl.ds(pl.multiple_of(j * LANES, LANES), LANES)
        d = dlow[:, pts].astype(BF16).astype(F32)
        plain = jnp.concatenate([pred[2 * j], pred[2 * j + 1]], axis=0) - bcol[0 : 2 * HALF, :]
        second = jnp.sum(d * plain, axis=0, keepdims=True) * (1.0 / H)
        second = jnp.transpose(jnp.broadcast_to(second, (LANES, LANES)))[:, 0:1]
        d = jnp.concatenate([d, jnp.zeros((16, LANES), F32)], axis=0)
        dunit = jnp.dot(jnp.transpose(d).astype(BF16), wgain[...], preferred_element_type=F32)
        inv = s_inv[pts, :]
        unit = (lat[pts, :].astype(F32) - s_mean[pts, :]) * inv
        out_lat[pts, :] = (inv * (dunit - unit * second)).astype(BF16)

    pl.loop(0, 1)(latent_block)
    core_copy.wait()

    for x in range(NX):
        sum_core[x] = full[core, x] + r_core[x]

    @pl.loop(1, NX)
    def _(i):
        k = (my_x + i) % NX
        remote(
            sum_core.at[k], r_x.at[my_x], x_send.at[k], x_recv.at[my_x], {"member": k * YLO + y_lo}
        ).start()

    r_x[my_x] = sum_core[my_x]
    pl.loop(1, 4)(latent_block)

    @pl.loop(1, NX)
    def _(i):
        k = (my_x + i) % NX
        remote(
            sum_core.at[k], r_x.at[k], x_send.at[k], x_recv.at[k], {"member": k * YLO + y_lo}
        ).wait()

    sum_x[...] = (r_x[0] + r_x[1]) + (r_x[2] + r_x[3])

    def at_y(k):
        return {"member": my_x * YLO + k % YLO, "dp": k // YLO}

    @pl.loop(1, NY)
    def _(i):
        k = (my_y + i) % NY
        remote(sum_x.at[k], r_y.at[my_y], y_send.at[k], y_recv.at[my_y], at_y(k)).start()

    r_y[my_y] = sum_x[my_y]
    pl.loop(4, 6)(latent_block)

    @pl.loop(1, NY)
    def _(i):
        k = (my_y + i) % NY
        remote(sum_x.at[k], r_y.at[k], y_send.at[k], y_recv.at[k], at_y(k)).wait()

    sum_y[...] = jnp.sum(r_y[...], axis=0)

    @pl.loop(1, NZ)
    def _(i):
        k = (my_z + i) % NZ
        remote(sum_y, r_z.at[my_z], z_send.at[k], z_recv.at[my_z], {"space": k * 2 + core}).start()

    r_z[my_z] = sum_y[...]
    pl.loop(6, 8)(latent_block)

    @pl.loop(1, NZ)
    def _(i):
        k = (my_z + i) % NZ
        remote(sum_y, r_z.at[k], z_send.at[k], z_recv.at[k], {"space": k * 2 + core}).wait()

    final[core, my_x, my_y] = jnp.sum(r_z[...], axis=0)

    @pl.loop(1, NY)
    def _(i):
        k = (my_y + i) % NY
        piece = final.at[core, my_x, my_y]
        remote(piece, piece, gy_send.at[k], gy_recv.at[my_y], at_y(k)).start()

    @pl.loop(1, NY)
    def _(i):
        k = (my_y + i) % NY
        remote(
            final.at[core, my_x, my_y], final.at[core, my_x, k], gy_send.at[k], gy_recv.at[k], at_y(k)
        ).wait()

    @pl.loop(1, NX)
    def _(i):
        k = (my_x + i) % NX
        piece = final.at[core, my_x]
        remote(piece, piece, gx_send.at[k], gx_recv.at[my_x], {"member": k * YLO + y_lo}).start()

    @pl.loop(1, NX)
    def _(i):
        k = (my_x + i) % NX
        remote(
            final.at[core, my_x], final.at[core, k], gx_send.at[k], gx_recv.at[k],
            {"member": k * YLO + y_lo},
        ).wait()

    last = remote(final.at[core], final.at[core], gc_sem.at[0], gc_sem.at[1], {"space": mate})
    last.start()
    last.wait_send()
    remote(final.at[core], final.at[1 - core], gc_sem.at[0], gc_sem.at[1], {"space": mate}).wait_recv()

    for y in range(NY):
        cols = slice(y * LANES, (y + 1) * LANES)
        acc = jnp.zeros((16, LANES), F32)
        for g in range(7):
            piece = final[g // 4, g % 4, y]
            top = min(16, C - g * 16)
            out_w[g * 16 : g * 16 + top, cols] = piece[0:top]
            acc = acc + piece * wpad[g * 16 : (g + 1) * 16, cols].astype(F32)
        out_g[0:1, cols] = jnp.sum(acc, axis=0, keepdims=True) / gain[0:1, cols]
    out_x[...] = final[1, 3, 0]


def shards(latent, target, weight, bias, gain, channel_weight, band_offsets, row_points):
    bands = lax.axis_size("space")
    band = lax.axis_index("space")
    row_ids = jnp.arange(row_points.shape[0], dtype=jnp.int32)
    in_band = (row_ids[None, :] >= band_offsets[:-1, None]) & (
        row_ids[None, :] < band_offsets[1:, None]
    )
    counts = jnp.sum(jnp.where(in_band, row_points[None, :], 0), axis=1)
    live_count = jnp.sum(jnp.where(jnp.arange(bands, dtype=jnp.int32) == band, counts, 0))
    total_live = jnp.sum(counts).astype(F32)
    live = (jnp.arange(PTS, dtype=jnp.int32) < live_count).astype(F32)
    vmem = pl.BlockSpec(memory_space=pltpu.VMEM)

    def buf(*shape, kind=F32):
        return pltpu.VMEM(shape, kind)

    def sems(n):
        return pltpu.SemaphoreType.DMA((n,))

    grad_x, sum_w, sum_g, extra = pl.pallas_call(
        kernel,
        name="crps_head",
        out_shape=(
            jax.ShapeDtypeStruct((PTS, H), BF16),
            jax.ShapeDtypeStruct((C, H), F32),
            jax.ShapeDtypeStruct((1, H), F32),
            jax.ShapeDtypeStruct((16, LANES), F32),
        ),
        in_specs=[vmem] * 7,
        out_specs=(vmem,) * 4,
        scratch_shapes=[
            buf(LANES, H, kind=BF16), buf(LANES, H, kind=BF16),
            buf(LANES, LANES), buf(LANES, LANES), buf(16, LANES), buf(2 * HALF, LANES),
            buf(LANES, LANES),
            buf(PTS, H, kind=BF16), buf(PTS, 1), buf(PTS, 1),
            buf(MEMBERS, HALF, LANES), buf(MEMBERS, HALF, LANES),
            buf(MEMBERS, HALF, LANES), buf(MEMBERS, HALF, LANES),
            buf(2 * HALF, PTS),
            buf(2, NX, NY, 16, LANES), buf(NX, NY, 16, LANES), buf(NX, NY, 16, LANES),
            buf(NX, NY, 16, LANES), buf(NY, 16, LANES), buf(NY, 16, LANES),
            buf(16, LANES), buf(NZ, 16, LANES), buf(2, NX, NY, 16, LANES),
            sems(MEMBERS), sems(MEMBERS), sems(MEMBERS), sems(MEMBERS), sems(2),
            sems(NX), sems(NX), sems(NY), sems(NY), sems(NZ), sems(NZ),
            sems(NY), sems(NY), sems(NX), sems(NX), sems(2),
        ],
        compiler_params=pltpu.CompilerParams(collective_id=0, has_side_effects=True),
    )(
        latent.reshape(PTS, H), target[0], weight, bias[None], gain[None], channel_weight[None],
        live[None],
    )
    batch = lax.axis_size("dp")
    loss = extra[1, 0] / (C * batch * total_live)
    return (grad_x[None, None], sum_w, extra[0, :C], sum_g[0], loss)


def solution(mesh):
    return jax.shard_map(
        shards,
        mesh=mesh,
        in_specs=(
            P("member", "dp", "space", None),
            P("dp", None, "space"),
            P(), P(), P(), P(), P(), P(),
        ),
        out_specs=(P("member", "dp", "space", None), P(), P(), P(), P()),
        check_vma=False,
    )
```

time: 468 us -> 86.8 us (0.19)
  waiting for transfers between devices: 319 us -> 0 us
  blocking collectives: 99.5 us -> 0 us
  Pallas kernels: 0 us -> 72.5 us
  between operations: 17.9 us -> 3.08 us
  other arithmetic: 15.5 us -> 3.24 us
  matrix products: 6.64 us -> 0 us
    psum x1 -> x0, waiting for transfers between devices: 160 us -> none  [shards(): lax.psum((grad_w, grad_b, grad_g, local_score), ('member', 'space', 'dp'))]
    all_gather x1 -> x0, waiting for transfers between devices: 159 us -> none  [shards(): piece = lax.all_gather(predicted[None], 'member', axis=0, tiled=True)]
    psum x1 -> x0, blocking collectives: 99.5 us -> none  [shards(): lax.psum((grad_w, grad_b, grad_g, local_score), ('member', 'space', 'dp'))]
    pallas_call x0 -> x1, Pallas kernels: none -> 72.5 us  [shards(): pl.pallas_call(kernel, name='crps_head', out_shape=(jax.ShapeDtypeStruct(...]
    reduce_sum x5 -> x1, other arithmetic: 9.41 us -> 1.36 us  [shards(): total_live = jnp.sum(counts).astype(F32)]
    dot_general x3 -> x0, matrix products: 6.64 us -> none  [the longest x1 3.42 us: shards(): jnp.einsum('bcp,ch->bph', dpred_low, weight, preferred_element_type=jnp.f...]
    broadcast_in_dim x1 -> x0, other arithmetic: 4.71 us -> none  [shards(): return (grad_x[None], sum_w, sum_b, sum_g, loss)]
  transfers between devices with their start and end apart: 2 -> 0, of which waited for: 2 -> 0; matrix products, arithmetic and copies ran while one was open for 2% -> 0% of each run, Pallas kernels for 0% -> 0%
where the time goes in v1:
time: 86.8 us; the launch traced here: 86.5 us
  Pallas kernels  72.5 us (84%)
  local copies, waits for them, and re-layouts  7.66 us (9%)
  other arithmetic  3.24 us (4%)
  between operations  3.08 us (4%)
    pallas_call x1, Pallas kernels, shards(): pl.pallas_call(kernel, name='crps_head', out_shape=(jax.ShapeDtypeStruct(...  72.5 us
    unnamed x7, local copies, waits for them, and re-layouts  4.49 us

profile of v1, /device:TPU:1, one launch (start us, length us, event | category | flops | bytes accessed | tf_op | source)
XLA Modules:
  0.0 86.5 jit_solution(5648181461422426958)
XLA Ops:
  0.6 0.8 fusion.2
  1.4 1.4 %select_reduce_fusion = (s32[]{:T(128)}, s32[16]{0:T(128)S(1)}) fusion(s32[128]{0:T(128)} %param.15, s32[16]{0:T(128)S(1)} %get-tuple-element.16, s32[16]{0:T(128)S(1)} %get-tuple-element.15), kind=kLoop, calls=%fused_computation.1 | loop fusion | flops 12271 | bytes 708 | tf_op jit(solution)/shard_map/reduce_sum | solution.py:301
  2.8 0.6 fusion.1
  3.4 1.2 %compare_convert_fusion.live = f32[1,1024]{1,0:T(1,128)} fusion(s32[]{:T(128)} %fusion.1), kind=kLoop, calls=%fused_computation | loop fusion | flops 2048 | bytes 4100 | tf_op jit(solution)/shard_map/convert_element_type | solution.py:302
  4.7 72.5 %crps_head.1 = (bf16[1024,1024]{1,0:T(8,128)(2,1)}, f32[100,1024]{1,0:T(8,128)}, f32[1,1024]{1,0:T(1,128)}, f32[16,128]{1,0:T(8,128)}) custom-call(bf16[1024,1024]{1,0:T(8,128)(2,1)} %bitcast.10, bf16[100,1024]{1,0:T(8,128)(2,1)} %bitcast.12, bf16[100,1024]{1,0:T(8,128)(2,1)} %weight.1, f32[1,100]{1,0:T(1,128)} %bitcast.15, f32[1,1024]{1,0:T(1,128)} %bitcast.13, ...), custom_call_target="tpu_custom_call" | custom-call | tf_op jit(solution)/shard_map/crps_head/pallas_call | solution.py:311
  77.2 1.2 %slice.15 = f32[1,1]{1,0:T(1,128)} slice(f32[16,128]{1,0:T(8,128)} %get-tuple-element.11), slice={[1:2], [0:1]} | slice | bytes 8 | tf_op jit(solution)/shard_map/slice | solution.py:343
  79.7 1.2 %slice_bitcast_fusion = f32[100]{0:T(128)} fusion(f32[16,128]{1,0:T(8,128)} %get-tuple-element.11), kind=kLoop, calls=%fused_computation.8 | loop fusion | bytes 800 | tf_op jit(solution)/shard_map/squeeze | solution.py:344
  80.9 0.0 copy-start
  80.9 0.0 copy-start.1
  80.9 3.1 %copy.16 = bf16[1,1,1024,1024]{3,2,1,0:T(8,128)(2,1)} copy(bf16[1,1,1024,1024]{3,2,1,0:T(8,128)(2,1)} %bitcast.11) | data formatting | bytes 4194304
  84.0 0.0 copy-done
  84.0 0.8 copy.17
  84.8 0.0 copy-done.1
  84.8 0.6 copy.18
Async XLA Ops:
  80.9 3.1 %copy-start = (f32[100,1024]{1,0:T(8,128)S(1)}, f32[100,1024]{1,0:T(8,128)}, u32[]{:S(2)}) copy-start(f32[100,1024]{1,0:T(8,128)} %get-tuple-element.23) | copy-start | bytes 1228804
  80.9 3.9 %copy-start.1 = (f32[1,1024]{1,0:T(1,128)S(1)}, f32[1,1024]{1,0:T(1,128)}, u32[]{:S(2)}) copy-start(f32[1,1024]{1,0:T(1,128)} %get-tuple-element.12) | copy-start | bytes 12292

commit v2 on v1

v2 whole, which is shorter than its diff:
```python
import jax
import jax.numpy as jnp
from jax import lax
from jax.experimental import pallas as pl
from jax.experimental.pallas import tpu as pltpu
from jax.sharding import PartitionSpec as P

MESH = pl.DeviceIdType.MESH
F32 = jnp.float32
BF16 = jnp.bfloat16
H, C, PTS = 1024, 100, 1024
MEMBERS, NX, NY, NZ, YLO = 16, 4, 8, 8, 4
HALF, LANES, BLOCKS, PIECES = 56, 128, 8, 7
SMOOTH = 0.01


def remote(src, dst, send, recv, where):
    return pltpu.make_async_remote_copy(
        src_ref=src, dst_ref=dst, send_sem=send, recv_sem=recv, device_id=where, device_id_type=MESH
    )


def kernel(
    lat_in, tgt, weight, bias, gain, chan, offsets, row_points,
    out_lat, out_w, out_g, out_b, out_loss,
    lat, tbuf,
    wpad, wgain, bcol, qcol, rows, tpad, bsum,
    scaled, s_mean, s_inv, pred, got, back, grads, dlow,
    full, r_core, sum_core, r_x, sum_x, r_y, sum_y, r_z, final,
    l_sem, t_sem, a_send, a_recv, b_send, b_recv, c_send, c_recv, x_send, x_recv, y_send, y_recv,
    z_send, z_recv, gy_send, gx_send, g_recv, gm_send, gm_recv,
):
    me = lax.axis_index("member")
    sp = lax.axis_index("space")
    dp = lax.axis_index("dp")
    my_x, y_lo = me // YLO, me % YLO
    my_y = dp * YLO + y_lo
    my_z, core = sp // 2, sp % 2
    far = (dp + 1) % 2
    mate = my_z * 2 + (1 - core)
    block, half = me // 2, me % 2

    barrier = pltpu.get_barrier_semaphore()

    @pl.loop(1, MEMBERS)
    def _(i):
        pl.semaphore_signal(barrier, inc=1, device_id={"member": (me + i) % MEMBERS}, device_id_type=MESH)

    @pl.loop(0, YLO)
    def _(i):
        pl.semaphore_signal(
            barrier, inc=1, device_id={"member": my_x * YLO + i, "dp": far}, device_id_type=MESH
        )

    @pl.loop(1, NZ)
    def _(i):
        pl.semaphore_signal(
            barrier, inc=1, device_id={"space": ((my_z + i) % NZ) * 2 + core}, device_id_type=MESH
        )

    pl.semaphore_signal(barrier, inc=1, device_id={"space": mate}, device_id_type=MESH)

    def load(i):
        j = (block + 1 + i) % BLOCKS
        pts = pl.ds(pl.multiple_of(j * LANES, LANES), LANES)
        return pltpu.make_async_copy(lat_in.at[pts, :], lat.at[pts, :], l_sem.at[j])

    @pl.loop(0, BLOCKS)
    def _(i):
        load(i).start()

    mine = pl.ds(pl.multiple_of(block * LANES, LANES), LANES)
    load_target = pltpu.make_async_copy(tgt.at[:, mine], tbuf, t_sem)
    load_target.start()

    wpad[96:128, :] = jnp.zeros((32, H), BF16)
    wpad[0:C, :] = weight[...]
    rows[...] = jnp.zeros((16, LANES), F32)
    rows[0:1, 0:C] = bias[...]
    rows[8:9, 0:C] = chan[...]
    bcol[...] = jnp.transpose(jnp.broadcast_to(rows[0:1, :], (LANES, LANES)))
    qcol[...] = jnp.transpose(jnp.broadcast_to(rows[8:9, :], (LANES, LANES)))
    pl.semaphore_wait(barrier, (MEMBERS - 1) + YLO + (NZ - 1) + 1)

    @pl.loop(0, BLOCKS)
    def _(i):
        j = (block + 1 + i) % BLOCKS
        pts = pl.ds(pl.multiple_of(j * LANES, LANES), LANES)
        load(i).wait()
        values = lat[pts, :].astype(F32)
        mean = jnp.sum(values, axis=1, keepdims=True) * (1.0 / H)
        centered = values - mean
        var = jnp.sum(centered * centered, axis=1, keepdims=True) * (1.0 / H)
        inv = lax.rsqrt(var + 1e-05)
        low = ((centered * inv) * gain[...]).astype(BF16)
        scaled[pts, :] = low
        s_mean[pts, :] = mean
        s_inv[pts, :] = inv
        out = lax.dot_general(
            wpad[0 : 2 * HALF, :], low, (((1,), (1,)), ((), ())), preferred_element_type=F32
        )
        out = out + bcol[0 : 2 * HALF, :]
        for r in range(2):
            k = 2 * j + r
            pred[k] = out[r * HALF : (r + 1) * HALF]

            @pl.when(k != me)
            def _():
                remote(pred.at[k], got.at[me], a_send.at[k], a_recv.at[me], {"member": k}).start()

    load_target.wait()
    tpad[96:112, :] = jnp.zeros((16, LANES), F32)
    tpad[0:C, :] = tbuf[...].astype(F32)
    bsum[...] = jnp.zeros((LANES, LANES), F32)
    got[me] = pred[me]

    row_ids = lax.broadcasted_iota(jnp.int32, (1, LANES), 1)
    counts = row_points[...].astype(F32)
    in_band = (row_ids >= offsets[sp]) & (row_ids < offsets[sp + 1])
    live_count = jnp.sum(jnp.where(in_band, counts, 0.0), axis=1, keepdims=True)
    total_live = jnp.sum(jnp.where(row_ids < offsets[16], counts, 0.0), axis=1, keepdims=True)
    live_row = ((row_ids + block * LANES).astype(F32) < live_count).astype(F32)

    wg = wpad[...].astype(F32) * gain[...]
    wgain[...] = (wg - jnp.sum(wg, axis=1, keepdims=True) * (1.0 / H)).astype(BF16)

    @pl.loop(1, MEMBERS)
    def _(i):
        k = (me + i) % MEMBERS
        remote(pred.at[k], got.at[k], a_send.at[k], a_recv.at[k], {"member": k}).wait()

    pair = 1.0 / (MEMBERS - 1)

    def tile(t, score):
        row = pl.multiple_of(t * 8, 8)
        here = pl.ds(row, 8)
        band = pl.ds(pl.multiple_of(half * HALF + row, 8), 8)
        q = qcol[band, :] * live_row
        obs = tpad[band, :]
        p = [got[m, here, :] for m in range(MEMBERS)]
        slope = [None] * MEMBERS
        spread = jnp.zeros((8, LANES), F32)
        for m in range(MEMBERS):
            for n in range(m + 1, MEMBERS):
                gap = p[m] - p[n]
                square = gap * gap + SMOOTH
                root = lax.rsqrt(square)
                spread = spread + square * root
                sign = gap * root
                slope[m] = sign if slope[m] is None else slope[m] + sign
                slope[n] = -sign if slope[n] is None else slope[n] - sign
        skill = jnp.zeros((8, LANES), F32)
        total = jnp.zeros((8, LANES), F32)
        for m in range(MEMBERS):
            gap = p[m] - obs
            square = gap * gap + SMOOTH
            root = lax.rsqrt(square)
            skill = skill + square * root
            sign = gap * root
            total = total + sign
            back[m, here, :] = q * (sign - pair * slope[m])
        bsum[band, :] = q * total
        return score + q * (skill - pair * spread)

    score = lax.fori_loop(0, HALF // 8, tile, jnp.zeros((8, LANES), F32))
    score = jnp.sum(jnp.sum(score, axis=1, keepdims=True), axis=0, keepdims=True)

    @pl.loop(1, MEMBERS)
    def _(i):
        k = (me + i) % MEMBERS
        remote(back.at[k], grads.at[me], b_send.at[k], b_recv.at[me], {"member": k}).start()

    grads[me] = back[me]
    bias_row = jnp.sum(jnp.transpose(bsum[...]), axis=0, keepdims=True)
    row_id = lax.broadcasted_iota(jnp.int32, (16, LANES), 0)
    extra = jnp.where(row_id == 4, bias_row, jnp.where(row_id == 5, score, 0.0))

    @pl.loop(1, MEMBERS)
    def _(i):
        k = (me + i) % MEMBERS
        remote(back.at[k], grads.at[k], b_send.at[k], b_recv.at[k], {"member": k}).wait()

    for j in range(BLOCKS):
        pts = slice(j * LANES, (j + 1) * LANES)
        dlow[0:HALF, pts] = grads[2 * j]
        dlow[HALF : 2 * HALF, pts] = grads[2 * j + 1]

    dl = dlow[...].astype(BF16)
    for tile_id in range(8):
        gw = jnp.dot(
            dl, scaled[:, tile_id * LANES : (tile_id + 1) * LANES], preferred_element_type=F32
        )
        for g in range(PIECES):
            piece = gw[g * 16 : (g + 1) * 16]
            if tile_id == 0 and g == 6:
                piece = piece + extra
            full[tile_id // 4, tile_id % 4, g] = piece

    def to_mate(x):
        return remote(
            full.at[1 - core, x], r_core.at[x], c_send.at[x], c_recv.at[x], {"space": mate}
        )

    def to_x(k, slot):
        return remote(
            sum_core.at[k], r_x.at[slot], x_send.at[k], x_recv.at[slot], {"member": k * YLO + y_lo}
        )

    @pl.loop(1, NX + 1)
    def _(i):
        to_mate((my_x + i) % NX).start()

    def latent_block(j):
        pts = pl.ds(pl.multiple_of(j * LANES, LANES), LANES)
        d = dlow[:, pts].astype(BF16).astype(F32)
        plain = jnp.concatenate([pred[2 * j], pred[2 * j + 1]], axis=0) - bcol[0 : 2 * HALF, :]
        second = jnp.sum(d * plain, axis=0, keepdims=True) * (1.0 / H)
        second = jnp.transpose(jnp.broadcast_to(second, (LANES, LANES)))[:, 0:1]
        d = jnp.concatenate([d, jnp.zeros((16, LANES), F32)], axis=0)
        dunit = jnp.dot(jnp.transpose(d).astype(BF16), wgain[...], preferred_element_type=F32)
        inv = s_inv[pts, :]
        unit = (lat[pts, :].astype(F32) - s_mean[pts, :]) * inv
        out_lat[pts, :] = (inv * (dunit - unit * second)).astype(BF16)

    pl.loop(0, 1)(latent_block)

    @pl.loop(1, NX)
    def _(i):
        k = (my_x + i) % NX
        to_mate(k).wait()
        sum_core[k] = full[core, k] + r_core[k]
        to_x(k, my_x).start()

    to_mate(my_x).wait()
    r_x[my_x] = full[core, my_x] + r_core[my_x]
    pl.loop(1, 4)(latent_block)

    @pl.loop(1, NX)
    def _(i):
        k = (my_x + i) % NX
        to_x(k, k).wait()

    sum_x[...] = (r_x[0] + r_x[1]) + (r_x[2] + r_x[3])

    def at_y(k):
        return {"member": my_x * YLO + k % YLO, "dp": k // YLO}

    owner = my_y < PIECES

    @pl.loop(1, NY)
    def _(i):
        k = (my_y + i) % NY

        @pl.when(k < PIECES)
        def _():
            remote(sum_x.at[k], r_y.at[my_y], y_send.at[k], y_recv.at[my_y], at_y(k)).start()

    pl.loop(4, 6)(latent_block)

    @pl.loop(1, NY)
    def _(i):
        k = (my_y + i) % NY

        @pl.when(k < PIECES)
        def _():
            remote(sum_x.at[k], r_y.at[my_y], y_send.at[k], y_recv.at[my_y], at_y(k)).wait_send()

        @pl.when(owner)
        def _():
            remote(sum_x.at[0], r_y.at[k], y_send.at[k], y_recv.at[k], at_y(k)).wait_recv()

    @pl.when(owner)
    def _():
        r_y[my_y] = sum_x[my_y]
        sum_y[...] = jnp.sum(r_y[...], axis=0)

        @pl.loop(1, NZ)
        def _(i):
            k = (my_z + i) % NZ
            remote(sum_y, r_z.at[my_z], z_send.at[k], z_recv.at[my_z], {"space": k * 2 + core}).start()

        r_z[my_z] = sum_y[...]

    pl.loop(6, 8)(latent_block)

    def spread_y(k):
        piece = final.at[core, my_x, my_y]
        return remote(piece, piece, gy_send.at[k], g_recv.at[my_x, my_y], at_y(k))

    def spread_x(k, x):
        piece = final.at[core, my_x, k]
        return remote(
            piece, piece, gx_send.at[x, k], g_recv.at[my_x, k], {"member": x * YLO + y_lo}
        )

    def arrived(x, k):
        piece = final.at[core, x, k]
        return remote(piece, piece, gy_send.at[0], g_recv.at[x, k], {"space": mate})

    def spread_mate(x, k):
        piece = final.at[core, x, k]
        return remote(piece, piece, gm_send.at[x, k], gm_recv.at[x, k], {"space": mate})

    def mate_arrived(x, k):
        piece = final.at[1 - core, x, k]
        return remote(piece, piece, gm_send.at[x, k], gm_recv.at[x, k], {"space": mate})

    @pl.when(owner)
    def _():
        @pl.loop(1, NZ)
        def _(i):
            k = (my_z + i) % NZ
            remote(sum_y, r_z.at[k], z_send.at[k], z_recv.at[k], {"space": k * 2 + core}).wait()

        final[core, my_x, my_y] = jnp.sum(r_z[...], axis=0)

        @pl.loop(1, NY)
        def _(i):
            spread_y((my_y + i) % NY).start()

    @pl.loop(0, NY)
    def _(i):
        k = (my_y + i) % NY

        @pl.when(k < PIECES)
        def _():
            @pl.when(i > 0)
            def _():
                arrived(my_x, k).wait_recv()

            @pl.loop(1, NX)
            def _(d):
                spread_x(k, (my_x + d) % NX).start()

            spread_mate(my_x, k).start()

    @pl.loop(0, NY)
    def _(i):
        k = (my_y + i) % NY

        @pl.when(k < PIECES)
        def _():
            @pl.loop(1, NX)
            def _(d):
                x = (my_x + d) % NX
                arrived(x, k).wait_recv()
                spread_mate(x, k).start()

    @pl.when(owner)
    def _():
        @pl.loop(1, NY)
        def _(i):
            spread_y((my_y + i) % NY).wait_send()

    @pl.loop(0, PIECES)
    def _(k):
        @pl.loop(1, NX)
        def _(d):
            spread_x(k, (my_x + d) % NX).wait_send()

        @pl.loop(0, NX)
        def _(x):
            spread_mate(x, k).wait_send()
            mate_arrived(x, k).wait_recv()

    for tile_id in range(8):
        cols = slice(tile_id * LANES, (tile_id + 1) * LANES)
        acc = jnp.zeros((16, LANES), F32)
        for g in range(PIECES):
            piece = final[tile_id // 4, tile_id % 4, g]
            top = min(16, C - g * 16)
            out_w[g * 16 : g * 16 + top, cols] = piece[0:top]
            acc = acc + piece * wpad[g * 16 : (g + 1) * 16, cols].astype(F32)
        out_g[0:1, cols] = jnp.sum(acc, axis=0, keepdims=True) / gain[0:1, cols]
    out_b[...] = final[0, 0, 6, 4:5, 0:C]
    out_loss[...] = final[0, 0, 6, 5:6, 0:1] / (C * 2.0 * total_live)


def shards(latent, target, weight, bias, gain, channel_weight, band_offsets, row_points):
    vmem = pl.BlockSpec(memory_space=pltpu.VMEM)

    def buf(*shape, kind=F32):
        return pltpu.VMEM(shape, kind)

    def sems(*shape):
        return pltpu.SemaphoreType.DMA(shape)

    hbm = pl.BlockSpec(memory_space=pl.ANY)
    smem = pl.BlockSpec(memory_space=pltpu.SMEM)
    grad_x, sum_w, sum_g, sum_b, loss = pl.pallas_call(
        kernel,
        name="crps_head",
        out_shape=(pltpu.VMEM((PTS, H), BF16), pltpu.VMEM((C, H), F32), pltpu.VMEM((1, H), F32), pltpu.VMEM((1, C), F32), pltpu.VMEM((1, 1), F32)),
        in_specs=[hbm, hbm, vmem, vmem, vmem, vmem, smem, vmem],
        out_specs=(vmem,) * 5,
        scratch_shapes=[
            buf(PTS, H, kind=BF16), buf(C, LANES, kind=BF16),
            buf(LANES, H, kind=BF16), buf(LANES, H, kind=BF16),
            buf(LANES, LANES), buf(LANES, LANES), buf(16, LANES), buf(2 * HALF, LANES),
            buf(LANES, LANES),
            buf(PTS, H, kind=BF16), buf(PTS, 1), buf(PTS, 1),
            buf(MEMBERS, HALF, LANES), buf(MEMBERS, HALF, LANES),
            buf(MEMBERS, HALF, LANES), buf(MEMBERS, HALF, LANES),
            buf(2 * HALF, PTS),
            buf(2, NX, PIECES, 16, LANES), buf(NX, PIECES, 16, LANES),
            buf(NX, PIECES, 16, LANES), buf(NX, PIECES, 16, LANES), buf(PIECES, 16, LANES),
            buf(NY, 16, LANES), buf(16, LANES), buf(NZ, 16, LANES), buf(2, NX, PIECES, 16, LANES),
            sems(BLOCKS), pltpu.SemaphoreType.DMA,
            sems(MEMBERS), sems(MEMBERS), sems(MEMBERS), sems(MEMBERS), sems(NX), sems(NX),
            sems(NX), sems(NX), sems(NY), sems(NY), sems(NZ), sems(NZ),
            sems(NY), sems(NX, PIECES), sems(NX, PIECES), sems(NX, PIECES), sems(NX, PIECES),
        ],
        compiler_params=pltpu.CompilerParams(collective_id=0, has_side_effects=True),
    )(
        latent.reshape(PTS, H), target[0], weight, bias[None], gain[None], channel_weight[None],
        band_offsets, row_points[None],
    )
    return (grad_x[None, None], sum_w, sum_b[0], sum_g[0], loss[0, 0])


def solution(mesh):
    return jax.shard_map(
        shards,
        mesh=mesh,
        in_specs=(
            P("member", "dp", "space", None),
            P("dp", None, "space"),
            P(), P(), P(), P(), P(), P(),
        ),
        out_specs=(P("member", "dp", "space", None), P(), P(), P(), P()),
        check_vma=False,
    )
```

time: 86.8 us -> 75 us (0.86)
  local copies, waits for them, and re-layouts: 7.66 us -> 3.18 us
  other arithmetic: 3.24 us -> 0 us
  Pallas kernels: 72.5 us -> 69.9 us
  between operations: 3.08 us -> 1.81 us
    pallas_call x1, Pallas kernels: 72.5 us -> 69.9 us  [shards(): pl.pallas_call(kernel, name='crps_head', out_shape=(pltpu.VMEM((PTS, H),...]
    reduce_sum x2 -> x0, other arithmetic: 1.99 us -> none  [the longest x1 1.36 us: shards(): total_live = jnp.sum(counts).astype(F32)]
    slice x2 -> x0, local copies, waits for them, and re-layouts: 1.99 us -> none  [the longest x1 1.18 us: shards(): loss = extra[1, 0] / (C * batch * total_live)]
    unnamed x7 -> x4, local copies, waits for them, and re-layouts: 4.49 us -> 3.18 us
    convert_element_type x1 -> x0, other arithmetic: 1.24 us -> none  [shards(): live = (jnp.arange(PTS, dtype=jnp.int32) < live_count).astype(F32)]
    squeeze x1 -> x0, local copies, waits for them, and re-layouts: 1.18 us -> none  [shards(): return (grad_x[None, None], sum_w, extra[0, :C], sum_g[0], loss)]
where the time goes in v2:
time: 75 us; the launch traced here: 74.9 us
  Pallas kernels  69.9 us (93%)
  local copies, waits for them, and re-layouts  3.18 us (4%)
  between operations  1.81 us (2%)
    pallas_call x1, Pallas kernels, shards(): pl.pallas_call(kernel, name='crps_head', out_shape=(pltpu.VMEM((PTS, H),...  69.9 us
    unnamed x4, local copies, waits for them, and re-layouts  3.18 us

profile of v2, /device:TPU:1, one launch (start us, length us, event | category | flops | bytes accessed | tf_op | source)
XLA Modules:
  0.0 74.9 jit_solution(4892199312031335084)
XLA Ops:
  0.6 69.9 %crps_head.1 = (bf16[1024,1024]{1,0:T(8,128)(2,1)S(1)}, f32[100,1024]{1,0:T(8,128)S(1)}, f32[1,1024]{1,0:T(1,128)S(1)}, f32[1,100]{1,0:T(1,128)S(1)}, f32[1,1]{1,0:T(1,128)S(1)}) custom-call(bf16[1024,1024]{1,0:T(8,128)(2,1)} %bitcast.13, bf16[100,1024]{1,0:T(8,128)(2,1)} %bitcast.14, bf16[100,1024]{1,0:T(8,128)(2,1)} %weight.1, f32[1,100]{1,0:T(1,128)} %bitcast.16, ...), custom_call_target="tpu_custom_call" | custom-call | tf_op jit(solution)/shard_map/crps_head/pallas_call | solution.py:390
  70.6 1.3 %copy.18 = bf16[1,1,1024,1024]{3,2,1,0:T(8,128)(2,1)} copy(bf16[1,1,1024,1024]{3,2,1,0:T(8,128)(2,1)S(1)} %bitcast.10) | data formatting | bytes 4194304
  71.9 0.5 copy.20
  72.4 0.6 copy.21
  73.0 0.8 %copy.19 = f32[100,1024]{1,0:T(8,128)} copy(f32[100,1024]{1,0:T(8,128)S(1)} %get-tuple-element.16) | data formatting | bytes 819200

commit v3 on v2

--- a/solution.py
+++ b/solution.py
@@ -10,7 +10,7 @@
 BF16 = jnp.bfloat16
 H, C, PTS = 1024, 100, 1024
 MEMBERS, NX, NY, NZ, YLO = 16, 4, 8, 8, 4
-HALF, LANES, BLOCKS, PIECES = 56, 128, 8, 7
+HALF, REST, LANES, BLOCKS, PIECES = 56, 48, 128, 8, 7
 SMOOTH = 0.01
 
 
@@ -28,7 +28,7 @@
     scaled, s_mean, s_inv, pred, got, back, grads, dlow,
     full, r_core, sum_core, r_x, sum_x, r_y, sum_y, r_z, final,
     l_sem, t_sem, a_send, a_recv, b_send, b_recv, c_send, c_recv, x_send, x_recv, y_send, y_recv,
-    z_send, z_recv, gy_send, gx_send, g_recv, gm_send, gm_recv,
+    z_send, z_recv, gy_send, gx_send, gr_send, g_recv, gm_send, gm_recv,
 ):
     me = lax.axis_index("member")
     sp = lax.axis_index("space")
@@ -60,8 +60,21 @@
 
     pl.semaphore_signal(barrier, inc=1, device_id={"space": mate}, device_id_type=MESH)
 
+    side = y_lo // 2
+
+    def block_at(i):
+        return ((my_x + i % 4 + i // 4) % NX) * 2 + (side + 1 + i // 4) % 2
+
+    def member_at(i):
+        q = i // 4
+        x = (my_x + i % 4 + q // 3) % NX
+        return x * YLO + ((side + 1 + q // 2) % 2) * 2 + (y_lo + q + q // 2) % 2
+
+    def part(ref, k, h):
+        return ref.at[k] if h == 0 else ref.at[k, 0:REST]
+
     def load(i):
-        j = (block + 1 + i) % BLOCKS
+        j = block_at(i)
         pts = pl.ds(pl.multiple_of(j * LANES, LANES), LANES)
         return pltpu.make_async_copy(lat_in.at[pts, :], lat.at[pts, :], l_sem.at[j])
 
@@ -84,7 +97,7 @@
 
     @pl.loop(0, BLOCKS)
     def _(i):
-        j = (block + 1 + i) % BLOCKS
+        j = block_at(i)
         pts = pl.ds(pl.multiple_of(j * LANES, LANES), LANES)
         load(i).wait()
         values = lat[pts, :].astype(F32)
@@ -106,7 +119,7 @@
 
             @pl.when(k != me)
             def _():
-                remote(pred.at[k], got.at[me], a_send.at[k], a_recv.at[me], {"member": k}).start()
+                remote(part(pred, k, r), part(got, me, r), a_send.at[k], a_recv.at[me], {"member": k}).start()
 
     load_target.wait()
     tpad[96:112, :] = jnp.zeros((16, LANES), F32)
@@ -124,10 +137,26 @@
     wg = wpad[...].astype(F32) * gain[...]
     wgain[...] = (wg - jnp.sum(wg, axis=1, keepdims=True) * (1.0 / H)).astype(BF16)
 
-    @pl.loop(1, MEMBERS)
-    def _(i):
-        k = (me + i) % MEMBERS
-        remote(pred.at[k], got.at[k], a_send.at[k], a_recv.at[k], {"member": k}).wait()
+    for h in range(2):
+
+        @pl.when(half == h)
+        def _():
+            @pl.loop(0, MEMBERS - 1)
+            def _(i):
+                k = member_at(i)
+                remote(
+                    part(pred, k, h), part(got, k, h), a_send.at[k], a_recv.at[k], {"member": k}
+                ).wait_recv()
+
+        @pl.loop(0, BLOCKS)
+        def _(i):
+            k = 2 * i + h
+
+            @pl.when(k != me)
+            def _():
+                remote(
+                    part(pred, k, h), part(got, k, h), a_send.at[k], a_recv.at[k], {"member": k}
+                ).wait_send()
 
     pair = 1.0 / (MEMBERS - 1)
 
@@ -162,28 +191,51 @@
         bsum[band, :] = q * total
         return score + q * (skill - pair * spread)
 
-    score = lax.fori_loop(0, HALF // 8, tile, jnp.zeros((8, LANES), F32))
+    score = lax.fori_loop(0, HALF // 8 - half, tile, jnp.zeros((8, LANES), F32))
     score = jnp.sum(jnp.sum(score, axis=1, keepdims=True), axis=0, keepdims=True)
 
-    @pl.loop(1, MEMBERS)
-    def _(i):
-        k = (me + i) % MEMBERS
-        remote(back.at[k], grads.at[me], b_send.at[k], b_recv.at[me], {"member": k}).start()
+    for h in range(2):
+
+        @pl.when(half == h)
+        def _():
+            @pl.loop(0, MEMBERS - 1)
+            def _(i):
+                k = member_at(i)
+                remote(
+                    part(back, k, h), part(grads, me, h), b_send.at[k], b_recv.at[me], {"member": k}
+                ).start()
 
     grads[me] = back[me]
     bias_row = jnp.sum(jnp.transpose(bsum[...]), axis=0, keepdims=True)
     row_id = lax.broadcasted_iota(jnp.int32, (16, LANES), 0)
     extra = jnp.where(row_id == 4, bias_row, jnp.where(row_id == 5, score, 0.0))
 
-    @pl.loop(1, MEMBERS)
-    def _(i):
-        k = (me + i) % MEMBERS
-        remote(back.at[k], grads.at[k], b_send.at[k], b_recv.at[k], {"member": k}).wait()
-
+    for h in range(2):
+
+        @pl.loop(0, BLOCKS)
+        def _(i):
+            k = 2 * i + h
+
+            @pl.when(k != me)
+            def _():
+                remote(
+                    part(back, k, h), part(grads, k, h), b_send.at[k], b_recv.at[k], {"member": k}
+                ).wait_recv()
+
+        @pl.when(half == h)
+        def _():
+            @pl.loop(0, MEMBERS - 1)
+            def _(i):
+                k = member_at(i)
+                remote(
+                    part(back, k, h), part(grads, k, h), b_send.at[k], b_recv.at[k], {"member": k}
+                ).wait_send()
+
+    dlow[HALF + REST : 2 * HALF, :] = jnp.zeros((HALF - REST, PTS), F32)
     for j in range(BLOCKS):
         pts = slice(j * LANES, (j + 1) * LANES)
         dlow[0:HALF, pts] = grads[2 * j]
-        dlow[HALF : 2 * HALF, pts] = grads[2 * j + 1]
+        dlow[HALF : HALF + REST, pts] = grads[2 * j + 1, 0:REST]
 
     dl = dlow[...].astype(BF16)
     for tile_id in range(8):
@@ -293,6 +345,16 @@
             piece, piece, gx_send.at[x, k], g_recv.at[my_x, k], {"member": x * YLO + y_lo}
         )
 
+    def relay_from(k):
+        return (my_x + 3 + 2 * (k % 2)) % NX
+
+    def relay(k):
+        x = (my_x + 1 + 2 * (k % 2)) % NX
+        piece = final.at[core, relay_from(k), k]
+        return remote(
+            piece, piece, gr_send.at[k], g_recv.at[relay_from(k), k], {"member": x * YLO + y_lo}
+        )
+
     def arrived(x, k):
         piece = final.at[core, x, k]
         return remote(piece, piece, gy_send.at[0], g_recv.at[x, k], {"space": mate})
@@ -328,7 +390,7 @@
             def _():
                 arrived(my_x, k).wait_recv()
 
-            @pl.loop(1, NX)
+            @pl.loop(1, NX, step=2)
             def _(d):
                 spread_x(k, (my_x + d) % NX).start()
 
@@ -340,11 +402,26 @@
 
         @pl.when(k < PIECES)
         def _():
-            @pl.loop(1, NX)
+            @pl.loop(1, NX, step=2)
             def _(d):
                 x = (my_x + d) % NX
                 arrived(x, k).wait_recv()
+
+                @pl.when(x == relay_from(k))
+                def _():
+                    relay(k).start()
+
                 spread_mate(x, k).start()
+
+    @pl.loop(0, NY)
+    def _(i):
+        k = (my_y + i) % NY
+
+        @pl.when(k < PIECES)
+        def _():
+            x = (my_x + 2) % NX
+            arrived(x, k).wait_recv()
+            spread_mate(x, k).start()
 
     @pl.when(owner)
     def _():
@@ -354,9 +431,11 @@
 
     @pl.loop(0, PIECES)
     def _(k):
-        @pl.loop(1, NX)
+        @pl.loop(1, NX, step=2)
         def _(d):
             spread_x(k, (my_x + d) % NX).wait_send()
+
+        relay(k).wait_send()
 
         @pl.loop(0, NX)
         def _(x):
@@ -408,7 +487,7 @@
             sems(BLOCKS), pltpu.SemaphoreType.DMA,
             sems(MEMBERS), sems(MEMBERS), sems(MEMBERS), sems(MEMBERS), sems(NX), sems(NX),
             sems(NX), sems(NX), sems(NY), sems(NY), sems(NZ), sems(NZ),
-            sems(NY), sems(NX, PIECES), sems(NX, PIECES), sems(NX, PIECES), sems(NX, PIECES),
+            sems(NY), sems(NX, PIECES), sems(PIECES), sems(NX, PIECES), sems(NX, PIECES), sems(NX, PIECES),
         ],
         compiler_params=pltpu.CompilerParams(collective_id=0, has_side_effects=True),
     )(

time: 75 us -> 76.4 us (1.019)
  Pallas kernels: 69.9 us -> 71.2 us
    pallas_call x1, Pallas kernels: 69.9 us -> 71.2 us  [shards(): pl.pallas_call(kernel, name='crps_head', out_shape=(pltpu.VMEM((PTS, H),...]
where the time goes in v3:
time: 76.4 us; the launch traced here: 76.2 us
  Pallas kernels  71.2 us (93%)
  local copies, waits for them, and re-layouts  3.18 us (4%)
  between operations  1.81 us (2%)
    pallas_call x1, Pallas kernels, shards(): pl.pallas_call(kernel, name='crps_head', out_shape=(pltpu.VMEM((PTS, H),...  71.2 us
    unnamed x4, local copies, waits for them, and re-layouts  3.18 us

profile of v3, /device:TPU:1, one launch (start us, length us, event | category | flops | bytes accessed | tf_op | source)
XLA Modules:
  0.0 76.2 jit_solution(1252645405886016306)
XLA Ops:
  0.6 71.2 %crps_head.1 = (bf16[1024,1024]{1,0:T(8,128)(2,1)S(1)}, f32[100,1024]{1,0:T(8,128)S(1)}, f32[1,1024]{1,0:T(1,128)S(1)}, f32[1,100]{1,0:T(1,128)S(1)}, f32[1,1]{1,0:T(1,128)S(1)}) custom-call(bf16[1024,1024]{1,0:T(8,128)(2,1)} %bitcast.13, bf16[100,1024]{1,0:T(8,128)(2,1)} %bitcast.14, bf16[100,1024]{1,0:T(8,128)(2,1)} %weight.1, f32[1,100]{1,0:T(1,128)} %bitcast.16, ...), custom_call_target="tpu_custom_call" | custom-call | tf_op jit(solution)/shard_map/crps_head/pallas_call | solution.py:469
  71.9 1.3 %copy.18 = bf16[1,1,1024,1024]{3,2,1,0:T(8,128)(2,1)} copy(bf16[1,1,1024,1024]{3,2,1,0:T(8,128)(2,1)S(1)} %bitcast.10) | data formatting | bytes 4194304
  73.2 0.5 copy.20
  73.7 0.6 copy.21
  74.3 0.8 copy.19

commit v4 on v2

--- a/solution.py
+++ b/solution.py
@@ -10,7 +10,7 @@
 BF16 = jnp.bfloat16
 H, C, PTS = 1024, 100, 1024
 MEMBERS, NX, NY, NZ, YLO = 16, 4, 8, 8, 4
-HALF, LANES, BLOCKS, PIECES = 56, 128, 8, 7
+HALF, REST, FIRST, LANES, BLOCKS, PIECES = 56, 48, 32, 128, 8, 7
 SMOOTH = 0.01
 
 
@@ -60,8 +60,44 @@
 
     pl.semaphore_signal(barrier, inc=1, device_id={"space": mate}, device_id_type=MESH)
 
+    def block_at(i):
+        return (block + 1 + i) % BLOCKS
+
+    def member_at(i):
+        return (me + 1 + i) % MEMBERS
+
+    def seg(ref, k, g, h):
+        return ref.at[k, 0:FIRST] if g == 0 else ref.at[k, FIRST : REST if h else HALF]
+
+    def ahead(g, k, slot, h):
+        return remote(
+            seg(pred, k, g, h), seg(got, slot, g, h), a_send.at[g, k], a_recv.at[g, slot], {"member": k}
+        )
+
+    def home(g, k, slot, h):
+        return remote(
+            seg(back, k, g, h), seg(grads, slot, g, h), b_send.at[g, k], b_recv.at[g, slot], {"member": k}
+        )
+
+    def peers(fn):
+        @pl.loop(0, MEMBERS - 1)
+        def _(i):
+            fn(member_at(i))
+
+    def by_half(fn):
+        for h in range(2):
+            pl.when(half == h)(lambda h=h: fn(h))
+
+    def by_peer(fn):
+        for h in range(2):
+
+            @pl.loop(0, BLOCKS)
+            def _(i):
+                k = (2 * (block + 1 + i) + h) % MEMBERS
+                pl.when(k != me)(lambda: fn(k, h))
+
     def load(i):
-        j = (block + 1 + i) % BLOCKS
+        j = block_at(i)
         pts = pl.ds(pl.multiple_of(j * LANES, LANES), LANES)
         return pltpu.make_async_copy(lat_in.at[pts, :], lat.at[pts, :], l_sem.at[j])
 
@@ -84,7 +120,7 @@
 
     @pl.loop(0, BLOCKS)
     def _(i):
-        j = (block + 1 + i) % BLOCKS
+        j = block_at(i)
         pts = pl.ds(pl.multiple_of(j * LANES, LANES), LANES)
         load(i).wait()
         values = lat[pts, :].astype(F32)
@@ -106,7 +142,13 @@
 
             @pl.when(k != me)
             def _():
-                remote(pred.at[k], got.at[me], a_send.at[k], a_recv.at[me], {"member": k}).start()
+                ahead(0, k, me, r).start()
+
+    @pl.loop(0, BLOCKS)
+    def _(i):
+        for h in range(2):
+            k = 2 * block_at(i) + h
+            pl.when(k != me)(lambda k=k, h=h: ahead(1, k, me, h).start())
 
     load_target.wait()
     tpad[96:112, :] = jnp.zeros((16, LANES), F32)
@@ -124,10 +166,7 @@
     wg = wpad[...].astype(F32) * gain[...]
     wgain[...] = (wg - jnp.sum(wg, axis=1, keepdims=True) * (1.0 / H)).astype(BF16)
 
-    @pl.loop(1, MEMBERS)
-    def _(i):
-        k = (me + i) % MEMBERS
-        remote(pred.at[k], got.at[k], a_send.at[k], a_recv.at[k], {"member": k}).wait()
+    peers(lambda k: ahead(0, k, k, 0).wait_recv())
 
     pair = 1.0 / (MEMBERS - 1)
 
@@ -162,28 +201,26 @@
         bsum[band, :] = q * total
         return score + q * (skill - pair * spread)
 
-    score = lax.fori_loop(0, HALF // 8, tile, jnp.zeros((8, LANES), F32))
+    score = lax.fori_loop(0, FIRST // 8, tile, jnp.zeros((8, LANES), F32))
+    peers(lambda k: home(0, k, me, 0).start())
+    by_half(lambda h: peers(lambda k: ahead(1, k, k, h).wait_recv()))
+    score = lax.fori_loop(FIRST // 8, HALF // 8 - half, tile, score)
+    by_half(lambda h: peers(lambda k: home(1, k, me, h).start()))
     score = jnp.sum(jnp.sum(score, axis=1, keepdims=True), axis=0, keepdims=True)
-
-    @pl.loop(1, MEMBERS)
-    def _(i):
-        k = (me + i) % MEMBERS
-        remote(back.at[k], grads.at[me], b_send.at[k], b_recv.at[me], {"member": k}).start()
 
     grads[me] = back[me]
     bias_row = jnp.sum(jnp.transpose(bsum[...]), axis=0, keepdims=True)
     row_id = lax.broadcasted_iota(jnp.int32, (16, LANES), 0)
     extra = jnp.where(row_id == 4, bias_row, jnp.where(row_id == 5, score, 0.0))
 
-    @pl.loop(1, MEMBERS)
-    def _(i):
-        k = (me + i) % MEMBERS
-        remote(back.at[k], grads.at[k], b_send.at[k], b_recv.at[k], {"member": k}).wait()
-
+    by_peer(lambda k, h: home(0, k, k, h).wait_recv())
+    by_peer(lambda k, h: home(1, k, k, h).wait_recv())
+
+    dlow[HALF + REST : 2 * HALF, :] = jnp.zeros((HALF - REST, PTS), F32)
     for j in range(BLOCKS):
         pts = slice(j * LANES, (j + 1) * LANES)
         dlow[0:HALF, pts] = grads[2 * j]
-        dlow[HALF : 2 * HALF, pts] = grads[2 * j + 1]
+        dlow[HALF : HALF + REST, pts] = grads[2 * j + 1, 0:REST]
 
     dl = dlow[...].astype(BF16)
     for tile_id in range(8):
@@ -223,6 +260,9 @@
         out_lat[pts, :] = (inv * (dunit - unit * second)).astype(BF16)
 
     pl.loop(0, 1)(latent_block)
+    for g in range(2):
+        by_peer(lambda k, h: ahead(g, k, k, h).wait_send())
+        by_half(lambda h: peers(lambda k: home(g, k, k, h).wait_send()))
 
     @pl.loop(1, NX)
     def _(i):
@@ -406,7 +446,7 @@
             buf(NX, PIECES, 16, LANES), buf(NX, PIECES, 16, LANES), buf(PIECES, 16, LANES),
             buf(NY, 16, LANES), buf(16, LANES), buf(NZ, 16, LANES), buf(2, NX, PIECES, 16, LANES),
             sems(BLOCKS), pltpu.SemaphoreType.DMA,
-            sems(MEMBERS), sems(MEMBERS), sems(MEMBERS), sems(MEMBERS), sems(NX), sems(NX),
+            sems(2, MEMBERS), sems(2, MEMBERS), sems(2, MEMBERS), sems(2, MEMBERS), sems(NX), sems(NX),
             sems(NX), sems(NX), sems(NY), sems(NY), sems(NZ), sems(NZ),
             sems(NY), sems(NX, PIECES), sems(NX, PIECES), sems(NX, PIECES), sems(NX, PIECES),
         ],

time: 75 us -> 72.5 us (0.967)
  Pallas kernels: 69.9 us -> 67.3 us
    pallas_call x1, Pallas kernels: 69.9 us -> 67.3 us  [shards(): pl.pallas_call(kernel, name='crps_head', out_shape=(pltpu.VMEM((PTS, H),...]
where the time goes in v4:
time: 72.5 us; the launch traced here: 72.3 us
  Pallas kernels  67.3 us (93%)
  local copies, waits for them, and re-layouts  3.18 us (4%)
  between operations  1.81 us (2%)
    pallas_call x1, Pallas kernels, shards(): pl.pallas_call(kernel, name='crps_head', out_shape=(pltpu.VMEM((PTS, H),...  67.3 us
    unnamed x4, local copies, waits for them, and re-layouts  3.18 us

profile of v4, /device:TPU:1, one launch (start us, length us, event | category | flops | bytes accessed | tf_op | source)
XLA Modules:
  0.0 72.3 jit_solution(8208561670640538964)
XLA Ops:
  0.6 67.3 %crps_head.1 = (bf16[1024,1024]{1,0:T(8,128)(2,1)S(1)}, f32[100,1024]{1,0:T(8,128)S(1)}, f32[1,1024]{1,0:T(1,128)S(1)}, f32[1,100]{1,0:T(1,128)S(1)}, f32[1,1]{1,0:T(1,128)S(1)}) custom-call(bf16[1024,1024]{1,0:T(8,128)(2,1)} %bitcast.13, bf16[100,1024]{1,0:T(8,128)(2,1)} %bitcast.14, bf16[100,1024]{1,0:T(8,128)(2,1)} %weight.1, f32[1,100]{1,0:T(1,128)} %bitcast.16, ...), custom_call_target="tpu_custom_call" | custom-call | tf_op jit(solution)/shard_map/crps_head/pallas_call | solution.py:430
  68.0 1.3 %copy.18 = bf16[1,1,1024,1024]{3,2,1,0:T(8,128)(2,1)} copy(bf16[1,1,1024,1024]{3,2,1,0:T(8,128)(2,1)S(1)} %bitcast.10) | data formatting | bytes 4194304
  69.3 0.5 copy.20
  69.8 0.6 copy.21
  70.4 0.8 %copy.19 = f32[100,1024]{1,0:T(8,128)} copy(f32[100,1024]{1,0:T(8,128)S(1)} %get-tuple-element.16) | data formatting | bytes 819200

commit v5 on v4

--- a/solution.py
+++ b/solution.py
@@ -323,6 +323,10 @@
 
     pl.loop(6, 8)(latent_block)
 
+    def nearest(i):
+        step = (i + 1) // 2
+        return (my_y + (i % 2) * step + (1 - i % 2) * (NY - step)) % NY
+
     def spread_y(k):
         piece = final.at[core, my_x, my_y]
         return remote(piece, piece, gy_send.at[k], g_recv.at[my_x, my_y], at_y(k))
@@ -360,7 +364,7 @@
 
     @pl.loop(0, NY)
     def _(i):
-        k = (my_y + i) % NY
+        k = nearest(i)
 
         @pl.when(k < PIECES)
         def _():
@@ -376,7 +380,7 @@
 
     @pl.loop(0, NY)
     def _(i):
-        k = (my_y + i) % NY
+        k = nearest(i)
 
         @pl.when(k < PIECES)
         def _():

time: 72.5 us -> 72.2 us (level)
  no operation moved by 1% of the time
where the time goes in v5:
time: 72.2 us; the launch traced here: 72.1 us
  Pallas kernels  67.1 us (93%)
  local copies, waits for them, and re-layouts  3.18 us (4%)
  between operations  1.81 us (3%)
    pallas_call x1, Pallas kernels, shards(): pl.pallas_call(kernel, name='crps_head', out_shape=(pltpu.VMEM((PTS, H),...  67.1 us
    unnamed x4, local copies, waits for them, and re-layouts  3.18 us

profile of v5, /device:TPU:1, one launch (start us, length us, event | category | flops | bytes accessed | tf_op | source)
XLA Modules:
  0.0 72.1 jit_solution(863756933586357720)
XLA Ops:
  0.6 67.1 %crps_head.1 = (bf16[1024,1024]{1,0:T(8,128)(2,1)S(1)}, f32[100,1024]{1,0:T(8,128)S(1)}, f32[1,1024]{1,0:T(1,128)S(1)}, f32[1,100]{1,0:T(1,128)S(1)}, f32[1,1]{1,0:T(1,128)S(1)}) custom-call(bf16[1024,1024]{1,0:T(8,128)(2,1)} %bitcast.13, bf16[100,1024]{1,0:T(8,128)(2,1)} %bitcast.14, bf16[100,1024]{1,0:T(8,128)(2,1)} %weight.1, f32[1,100]{1,0:T(1,128)} %bitcast.16, ...), custom_call_target="tpu_custom_call" | custom-call | tf_op jit(solution)/shard_map/crps_head/pallas_call | solution.py:434
  67.7 1.3 %copy.18 = bf16[1,1,1024,1024]{3,2,1,0:T(8,128)(2,1)} copy(bf16[1,1,1024,1024]{3,2,1,0:T(8,128)(2,1)S(1)} %bitcast.10) | data formatting | bytes 4194304
  69.1 0.5 copy.20
  69.6 0.6 copy.21
  70.2 0.8 %copy.19 = f32[100,1024]{1,0:T(8,128)} copy(f32[100,1024]{1,0:T(8,128)S(1)} %get-tuple-element.16) | data formatting | bytes 819200
